TPU v7x, 256 devices: a whole 4x4x8 slice. The times are simulated.
256 devices in a mesh: dp: 8 (over x, core), seq: 32 (over z, y).
Axes of the slice: x: 4, y: 4, z: 8, core: 2. Of those that a mesh axis runs over, the one named last changes fastest.
Arguments:
- queries: bfloat16 [8, 8192, 2048], P('dp', 'seq'), may hold values from -40 to 40
- keys: bfloat16 [8, 8192, 2048], P('dp', 'seq'), may hold values from -40 to 40
- values: bfloat16 [8, 8192, 2048], P('dp', 'seq'), may hold values from -6 to 6
- key_gain: float32 [2048], replicated, may hold values from 0.25 to 1.75
- random_blocks: int32 [16, 128, 3], P(None, 'seq'), may hold values from 2 to 127, as said below
- out_grad: bfloat16 [8, 8192, 2048], P('dp', 'seq'), may hold values from -6 to 6
Outputs:
- attended: bfloat16 [8, 8192, 2048], P('dp', 'seq')
- query_grad: bfloat16 [8, 8192, 2048], P('dp', 'seq')
- key_grad: bfloat16 [8, 8192, 2048], P('dp', 'seq')
- value_grad: bfloat16 [8, 8192, 2048], P('dp', 'seq')
- gain_grad: float32 [2048], replicated
Inputs may be any that keep to these rules, and one draw needn't show every extreme that they name: `random_blocks`: for the 4 query blocks of one device, all heads and entries together, at most 9 entries name blocks held by any one device (blocks d * 4 to d * 4 + 3), and exactly 9 name the blocks of some device.
All inputs are finite; a program needn't handle non-finite values.
Results may differ from a plain program's by a relative error of at most 0.03.
The roundings to bfloat16 on the way count: a program that leaves them out, or rounds other values in their place, can miss the bound.
Values may be sent and summed in bfloat16 or wider, within the bound.
No kernel may reach another device: no remote copies, remote signals or barrier semaphores. Data moves between devices by JAX's collectives and lax.ppermute only.
A program may use at most 128 MiB of HBM per device.

v0:
```python
import math
import jax
import jax.numpy as jnp
from jax import lax
from jax.sharding import PartitionSpec as P

HEADS = 16
HD = 128
BLOCK = 64
NG = 2
NR = 3
NK = 8
NEGATIVE = -1e30


def broadcast(block, axis, owner):
    block = jnp.where(lax.axis_index(axis) == owner, block, jnp.zeros_like(block))
    return lax.psum(block, axis)


def padded_2(cells, sides, width):
    for axis, dim in sides:
        count = lax.axis_size(axis)
        ends = count - 1
        head = lax.slice_in_dim(cells, 0, width, axis=dim)
        tail = lax.slice_in_dim(cells, cells.shape[dim] - width, cells.shape[dim], axis=dim)
        cells = jnp.concatenate(
            [
                lax.ppermute(tail, axis, [(i, (i + 1) % count) for i in range(ends)]),
                cells,
                lax.ppermute(head, axis, [((i + 1) % count, i) for i in range(ends)]),
            ],
            axis=dim,
        )
    return cells


def passed_along(array, axis, by):
    length = lax.axis_size(axis)
    pairs = [(i, i + by) for i in range(length) if 0 <= i + by < length]
    return lax.ppermute(array, axis, pairs)


def to_heads(rows_in):
    return rows_in.reshape(rows_in.shape[0] // BLOCK, BLOCK, HEADS, HD).transpose(2, 0, 1, 3)


def from_heads(blocks_in):
    return blocks_in.transpose(1, 2, 0, 3).reshape(1, blocks_in.shape[1] * BLOCK, HEADS * HD)


def build_list(edge_part, window_part, random_in):
    head_count = random_in.shape[0]
    block_count = random_in.shape[1]
    global_list = jnp.broadcast_to(
        edge_part[:, None], (head_count, block_count) + edge_part.shape[1:]
    )
    window_list = jnp.stack(
        [window_part[:, offset : offset + block_count] for offset in range(3)], axis=2
    )
    joined = jnp.concatenate([global_list, window_list, random_in], axis=2)
    return joined.reshape(head_count, block_count, NK * BLOCK, HD)


def spread_terms(coef, rows_in):
    head_count = rows_in.shape[0]
    block_count = rows_in.shape[1]
    coef_blocks = coef.reshape(head_count, block_count, BLOCK, NK, BLOCK)
    global_term = jnp.einsum(
        "hpbgc,hpbd->hgcd", coef_blocks[:, :, :, :NG], rows_in, preferred_element_type=jnp.float32
    )
    padded = jnp.zeros((head_count, block_count + 2, BLOCK, HD), jnp.float32)
    for offset in range(3):
        term = jnp.einsum(
            "hpbc,hpbd->hpcd",
            coef_blocks[:, :, :, NG + offset],
            rows_in,
            preferred_element_type=jnp.float32,
        )
        padded = padded + jnp.pad(term, ((0, 0), (offset, 2 - offset), (0, 0), (0, 0)))
    random_term = jnp.einsum(
        "hpbrc,hpbd->hprcd",
        coef_blocks[:, :, :, NG + 3 :],
        rows_in,
        preferred_element_type=jnp.float32,
    )
    return (global_term, padded, random_term)


def sparse_group(
    query_blk,
    edge_key,
    edge_value,
    window_key,
    window_value,
    random_key,
    random_value,
    grad_blk,
    valid_keys,
    keep_rows,
):
    score_scale = HD ** (-0.5)
    key_list = build_list(edge_key, window_key, random_key)
    value_list = build_list(edge_value, window_value, random_value)
    key_mask = jnp.repeat(valid_keys, BLOCK, axis=1)[None, :, None, :]
    scores = (
        jnp.einsum("hpbd,hpnd->hpbn", query_blk, key_list, preferred_element_type=jnp.float32)
        * score_scale
    )
    scores = jnp.where(key_mask, scores, NEGATIVE)
    row_top = jnp.max(scores, axis=3, keepdims=True)
    expo_vals = jnp.where(key_mask, jnp.exp(scores - row_top), 0.0)
    row_total = jnp.sum(expo_vals, axis=3, keepdims=True)
    numerator = jnp.einsum(
        "hpbn,hpnd->hpbd",
        expo_vals.astype(jnp.bfloat16),
        value_list,
        preferred_element_type=jnp.float32,
    )
    attended = (numerator / row_total).astype(jnp.bfloat16)
    row_delta = jnp.sum(grad_blk.astype(jnp.float32) * attended.astype(jnp.float32), axis=3)
    weights = expo_vals / row_total * keep_rows[None, :, None, None]
    dprobs = jnp.einsum("hpbd,hpnd->hpbn", grad_blk, value_list, preferred_element_type=jnp.float32)
    dscores = (weights * (dprobs - row_delta[:, :, :, None]) * score_scale).astype(jnp.bfloat16)
    dquery = jnp.einsum("hpbn,hpnd->hpbd", dscores, key_list, preferred_element_type=jnp.float32)
    key_global, key_padded, key_random = spread_terms(dscores, query_blk)
    value_global, value_padded, value_random = spread_terms(weights.astype(jnp.bfloat16), grad_blk)
    global_part = jnp.stack([key_global, value_global], axis=1)
    padded = jnp.stack([key_padded, value_padded], axis=1)
    random_part = jnp.stack([key_random, value_random], axis=1)
    return (attended, dquery, global_part, padded, random_part)


def shards(queries, keys, values, key_gain, random_blocks, out_grad):
    score_scale = HD ** (-0.5)
    tok_count = queries.shape[1]
    per_dev = tok_count // BLOCK
    owners = lax.axis_size("seq")
    seq_place = lax.axis_index("seq")
    total_blocks = owners * per_dev
    first_block = seq_place * per_dev
    key_eff = (keys[0].astype(jnp.float32) * key_gain).astype(jnp.bfloat16)
    edge_count = NG * BLOCK
    edge_rows = broadcast(
        jnp.stack(
            [
                queries[0, :edge_count],
                key_eff[:edge_count],
                values[0, :edge_count],
                out_grad[0, :edge_count],
            ]
        ),
        "seq",
        0,
    )
    window_rows = padded_2(jnp.stack([key_eff, values[0]]), (("seq", 1),), BLOCK)
    query_h = to_heads(queries[0])
    key_h = to_heads(key_eff)
    value_h = to_heads(values[0])
    grad_h = to_heads(out_grad[0])
    edge_heads = [to_heads(edge_rows[slot_pick]) for slot_pick in range(4)]
    window_key = to_heads(window_rows[0])
    window_value = to_heads(window_rows[1])
    request_count = HEADS * per_dev * NR
    capacity = (request_count + owners - 1) // owners + 3
    target = random_blocks.reshape(request_count)
    owner_dev = target // per_dev
    table_index = (
        jnp.arange(request_count, dtype=jnp.int32) // (per_dev * NR) * per_dev + target % per_dev
    )
    onehot = (owner_dev[:, None] == jnp.arange(owners, dtype=jnp.int32)[None, :]).astype(jnp.int32)
    before = jnp.cumsum(onehot, axis=0) - onehot
    slot_rank = jnp.sum(before * onehot, axis=1)
    position = owner_dev * capacity + slot_rank
    outgoing = (
        jnp.full((owners * capacity,), -1, jnp.int32)
        .at[position]
        .set(table_index)
        .reshape(owners, capacity)
    )
    kv_table = jnp.concatenate([key_h, value_h], axis=3).reshape(HEADS * per_dev, BLOCK, 2 * HD)
    index_part = lax.all_to_all(outgoing, "seq", split_axis=0, concat_axis=0, tiled=True)
    picked = kv_table[jnp.clip(index_part, 0, HEADS * per_dev - 1)]
    fetch_result = (
        lax.all_to_all(picked, "seq", split_axis=0, concat_axis=0, tiled=True),
        index_part,
    )
    arrived, served = fetch_result
    fetched = arrived.reshape(owners * capacity, BLOCK, 2 * HD)[position].reshape(
        HEADS, per_dev, NR, BLOCK, 2 * HD
    )
    fetched_key = fetched[..., :HD]
    fetched_value = fetched[..., HD:]
    block_index = first_block + jnp.arange(per_dev, dtype=jnp.int32)
    window_index = block_index[:, None] + jnp.arange(-1, 2, dtype=jnp.int32)[None, :]
    valid_keys = jnp.concatenate(
        [
            jnp.ones((per_dev, NG), bool),
            (window_index >= NG) & (window_index < total_blocks),
            jnp.ones((per_dev, NR), bool),
        ],
        axis=1,
    )
    keep_rows = (block_index >= NG).astype(jnp.float32)
    group_size = math.gcd(HEADS, 4)

    def by_group(array_in):
        return array_in.reshape((HEADS // group_size, group_size) + array_in.shape[1:])

    def merge_groups(array_in):
        return array_in.reshape((HEADS,) + array_in.shape[2:])

    def run_group(bundle):
        return sparse_group(
            bundle[0],
            bundle[1],
            bundle[2],
            bundle[3],
            bundle[4],
            bundle[5],
            bundle[6],
            bundle[7],
            valid_keys,
            keep_rows,
        )

    grouped = lax.map(
        run_group,
        (
            by_group(query_h),
            by_group(edge_heads[1]),
            by_group(edge_heads[2]),
            by_group(window_key),
            by_group(window_value),
            by_group(fetched_key),
            by_group(fetched_value),
            by_group(grad_h),
        ),
    )
    attended_h, dquery_h, global_part, padded, random_part = [
        merge_groups(piece_out) for piece_out in grouped
    ]
    edge_query = edge_heads[0].reshape(HEADS, edge_count, HD)
    edge_grad = edge_heads[3].reshape(HEADS, edge_count, HD)
    flat_key = key_h.reshape(HEADS, tok_count, HD)
    flat_value = value_h.reshape(HEADS, tok_count, HD)
    edge_scores = (
        jnp.einsum("hqd,htd->hqt", edge_query, flat_key, preferred_element_type=jnp.float32)
        * score_scale
    )
    edge_top = lax.pmax(jnp.max(edge_scores, axis=2), "seq")
    edge_expo = jnp.exp(edge_scores - edge_top[:, :, None])
    edge_total, edge_numer = lax.psum(
        (
            jnp.sum(edge_expo, axis=2),
            jnp.einsum(
                "hqt,htd->hqd",
                edge_expo.astype(jnp.bfloat16),
                flat_value,
                preferred_element_type=jnp.float32,
            ),
        ),
        "seq",
    )
    edge_out = (edge_numer / edge_total[:, :, None]).astype(jnp.bfloat16)
    edge_delta = jnp.sum(edge_grad.astype(jnp.float32) * edge_out.astype(jnp.float32), axis=2)
    edge_weights = edge_expo / edge_total[:, :, None]
    edge_dprobs = jnp.einsum(
        "hqd,htd->hqt", edge_grad, flat_value, preferred_element_type=jnp.float32
    )
    edge_dscores = (edge_weights * (edge_dprobs - edge_delta[:, :, None]) * score_scale).astype(
        jnp.bfloat16
    )
    edge_dquery = jnp.einsum(
        "hqt,htd->hqd", edge_dscores, flat_key, preferred_element_type=jnp.float32
    )
    local_dkey = jnp.einsum(
        "hqt,hqd->htd", edge_dscores, edge_query, preferred_element_type=jnp.float32
    )
    local_dvalue = jnp.einsum(
        "hqt,hqd->htd",
        edge_weights.astype(jnp.bfloat16),
        edge_grad,
        preferred_element_type=jnp.float32,
    )
    random_rounded = (
        random_part.transpose(0, 2, 3, 4, 1, 5)
        .reshape(request_count, BLOCK, 2 * HD)
        .astype(jnp.bfloat16)
    )
    sendback = (
        jnp.zeros((owners * capacity, BLOCK, 2 * HD), jnp.bfloat16)
        .at[position]
        .set(random_rounded)
        .reshape(owners, capacity, BLOCK, 2 * HD)
    )
    returned = lax.all_to_all(sendback, "seq", split_axis=0, concat_axis=0, tiled=True)
    owner_table = (
        served.reshape(1, owners * capacity)
        == jnp.arange(HEADS * per_dev, dtype=jnp.int32)[:, None]
    ).astype(jnp.bfloat16)
    summed = jnp.dot(
        owner_table,
        returned.reshape(owners * capacity, BLOCK * 2 * HD),
        preferred_element_type=jnp.float32,
    )
    summed = summed.reshape(HEADS, per_dev, BLOCK, 2, HD).transpose(0, 3, 1, 2, 4)
    from_right = passed_along(padded[:, :, 0].astype(jnp.bfloat16), "seq", -1).astype(jnp.float32)
    from_left = passed_along(padded[:, :, per_dev + 1].astype(jnp.bfloat16), "seq", 1).astype(
        jnp.float32
    )
    edge_dquery_sum, global_sum = lax.psum((edge_dquery, global_part), "seq")
    accum = padded[:, :, 1 : per_dev + 1]
    accum = accum + jnp.stack([local_dkey, local_dvalue], axis=1).reshape(
        HEADS, 2, per_dev, BLOCK, HD
    )
    accum = accum + summed
    accum = accum.at[:, :, per_dev - 1].add(from_right)
    accum = accum.at[:, :, 0].add(from_left)
    is_first = (seq_place == 0).astype(jnp.float32)
    accum = accum.at[:, :, :NG].add(global_sum * is_first)
    is_edge = (block_index < NG)[None, :, None, None]
    tail_zeros = jnp.zeros((HEADS, per_dev - NG, BLOCK, HD), jnp.float32)
    edge_dq_blocks = jnp.concatenate(
        [edge_dquery_sum.reshape(HEADS, NG, BLOCK, HD), tail_zeros], axis=1
    )
    edge_out_blocks = jnp.concatenate(
        [edge_out.reshape(HEADS, NG, BLOCK, HD), tail_zeros.astype(jnp.bfloat16)], axis=1
    )
    dquery_all = jnp.where(is_edge, edge_dq_blocks, dquery_h).astype(jnp.bfloat16)
    attended_all = jnp.where(is_edge, edge_out_blocks, attended_h)
    key_eff_grad = accum[:, 0]
    gain_heads = key_gain.reshape(HEADS, HD)
    key_grad_h = (key_eff_grad * gain_heads[:, None, None, :]).astype(jnp.bfloat16)
    value_grad_h = accum[:, 1].astype(jnp.bfloat16)
    gain_term = jnp.sum(key_eff_grad * to_heads(keys[0]).astype(jnp.float32), axis=(1, 2)).reshape(
        HEADS * HD
    )
    gain_grad = lax.psum(gain_term, ("dp", "seq"))
    return (
        from_heads(attended_all),
        from_heads(dquery_all),
        from_heads(key_grad_h),
        from_heads(value_grad_h),
        gain_grad,
    )


def solution(mesh):
    placed = (
        P("dp", "seq", None),
        P("dp", "seq", None),
        P("dp", "seq", None),
        P(),
        P(None, "seq", None),
        P("dp", "seq", None),
    )
    return jax.shard_map(
        shards,
        mesh=mesh,
        in_specs=placed,
        out_specs=(
            P("dp", "seq", None),
            P("dp", "seq", None),
            P("dp", "seq", None),
            P("dp", "seq", None),
            P(),
        ),
        check_vma=False,
    )
```

profile of v0, /device:TPU:1, one launch (start us, length us, event | category | flops | bytes accessed | tf_op | source)
XLA Modules:
  0.0 1441.6 jit_solution(389370633972243564)
XLA Ops:
  11.2 12.0 all-to-all-start
  33.7 10.3 gather_fusion
  43.9 7.5 all-to-all-start.1
  68.2 25.1 %collective-permute-done = bf16[2,64,2048]{2,1,0:T(8,128)(2,1)} collective-permute-done((bf16[2,64,2048]{2,1,0:T(8,128)(2,1)}, bf16[2,64,2048]{2,1,0:T(8,128)(2,1)}, u32[]{:S(2)}, u32[]{:S(2)}) %collective-permute-start) | collective-permute-done | bytes 524320 | tf_op jit(solution)/shard_map/ppermute | solution.py:29
  93.3 21.3 %collective-permute-done.1 = bf16[2,64,2048]{2,1,0:T(8,128)(2,1)} collective-permute-done((bf16[2,64,2048]{2,1,0:T(8,128)(2,1)}, bf16[2,64,2048]{2,1,0:T(8,128)(2,1)}, u32[]{:S(2)}, u32[]{:S(2)}) %collective-permute-start.1) | collective-permute-done | bytes 524320 | tf_op jit(solution)/shard_map/ppermute | solution.py:31
  119.1 206.0 %all-reduce.14.cloned.1.call-done = bf16[4,128,2048]{2,1,0:T(8,128)(2,1)} async-done(((bf16[4,128,2048]{2,1,0:T(8,128)(2,1)}), bf16[4,128,2048]{2,1,0:T(8,128)(2,1)}) %all-reduce.14.cloned.1.call-update) | async-done | bytes 2097168 | tf_op jit(solution)/shard_map/psum | solution.py:18
  329.1 11.8 gather_fusion.1
  340.9 8.0 fusion.134
  348.9 287.8 %while.24 = (s32[]{:T(128)}, bf16[4,4,4,64,128]{4,3,2,1,0:T(8,128)(2,1)}, bf16[4,4,4,64,128]{4,3,2,1,0:T(8,128)(2,1)}, f32[4,4,2,2,64,128]{5,1,0,2,4,3:T(4,128)}...) while((s32[]{:T(128)}, ...), condition=%wide.region_14.15_spmd.clone, body=%wide.region_10.14_spmd.clone.sunk | while | flops 952370176 | bytes 142396560 | solution.py:227
  368.6 5.1 bitcast_dynamic-update-slice_fusion.6
  440.4 5.1 bitcast_dynamic-update-slice_fusion.6
  584.1 5.1 bitcast_dynamic-update-slice_fusion.6
  636.7 12.7 copy.168
  649.4 10.8 reshape.529
  665.1 29.1 %scatter_fusion = bf16[288,64,256]{2,1,0:T(8,128)(2,1)} fusion(bf16[288,64,256]{2,1,0:T(8,128)(2,1)} %broadcast_in_dim.167, s32[192]{0:T(256)S(1)} %bitcast.511, bf16[192,64,256]{2,1,0:T(8,128)(2,1)} %reshape.529), kind=kCustom, calls=%fused_computation.3 | custom fusion | bytes 18875136 | tf_op jit(solution)/shard_map/scatter | solution.py:294
  694.3 6.0 all-to-all-start.2
  704.3 248.7 %pmax.7 = f32[16,128]{1,0:T(8,128)S(1)} all-reduce(f32[16,128]{1,0:T(8,128)S(1)} %get-tuple-element.352), channel_id=1, replica_groups=mesh['dp'=8,'seq'=32] {'seq'}, use_global_device_ids=true, to_apply=%region_2.3 | all-reduce | flops 2048 | bytes 16384 | tf_op jit(solution)/shard_map/pmax | solution.py:251
  960.4 59.2 %psum.44 = f32[16,128]{1,0:T(8,128)S(1)} all-reduce(f32[16,128]{1,0:T(8,128)S(1)} %fusion.95), channel_id=1, replica_groups=mesh['dp'=8,'seq'=32] {'seq'}, use_global_device_ids=true, to_apply=%region_5.6 | all-reduce | flops 2048 | bytes 16384 | tf_op jit(solution)/shard_map/psum | solution.py:253
  1033.0 99.2 %all-reduce.16.cloned.1.call-done = (f32[16,128,128]{2,1,0:T(8,128)}, f32[16,2,2,64,128]{4,0,1,3,2:T(8,128)}) async-done(((f32[16,128,128]{2,1,0:T(8,128)}, f32[16,2,2,64,128]{4,0,1,3,2:T(8,128)}), (f32[16,128,128]{2,1,0:T(8,128)}, f32[16,2,2,64,128]{4,0,1,3,2:T(8,128)})) %all-reduce.16.cloned.1.call-update) | async-done | bytes 3145744 | tf_op jit(solution)/shard_map/psum | solution.py:253
  1141.9 123.4 %all-reduce.17 = bf16[16,2,64,128]{3,2,1,0:T(8,128)(2,1)S(1)} all-reduce(f32[16,2,64,128]{3,2,1,0:T(8,128)} %bitcast.485), channel_id=1, replica_groups=mesh['dp'=8,'seq'=32] {'seq'}, use_global_device_ids=true, to_apply=%region_16.17 | all-reduce | flops 262144 | bytes 1572864 | tf_op jit(solution)/shard_map/psum | solution.py:312
  1273.5 18.5 %copy.212 = bf16[36,8,64,256]{3,1,2,0:T(8,128)(2,1)} copy(bf16[36,8,64,256]{3,2,1,0:T(8,128)(2,1)} %bitcast.182) | data formatting | bytes 18874368
  1292.0 16.1 %dot_general.116 = bf16[64,2,128,288]{2,1,0,3:T(2,128)(2,1)} reshape(bf16[16384,288]{0,1:T(8,128)(2,1)} %bitcast.460) | data formatting | bytes 18874368 | tf_op jit(solution)/shard_map/dot_general | solution.py:302
  1308.1 12.3 fusion.85
  1328.3 106.2 %psum.47 = f32[2048]{0:T(1024)} all-reduce(f32[2048]{0:T(1024)S(1)} %bitcast.508), channel_id=1, replica_groups=mesh['dp'=8,'seq'=32] {'dp','seq'}, use_global_device_ids=true, to_apply=%region_20.21 | all-reduce | flops 2048 | bytes 16384 | tf_op jit(solution)/shard_map/psum | solution.py:339
  (477 shorter events, 365.1 us)
Async XLA Ops:
  9.3 58.8 %copy-start.31 = (s32[192,1]{0,1:T(1,128)}, s32[192,1]{0,1:T(1,128)S(1)}, u32[]{:S(2)}) copy-start(s32[192,1]{0,1:T(1,128)S(1)} %compare_select_fusion.1) | copy-start | bytes 2308
  11.2 20.6 %all-to-all-start = ((s32[32,1,9]{2,1,0:T(1,128)}), s32[32,1,9]{2,1,0:T(1,128)S(1)}, u32[]{:S(2)}, u32[]{:S(2)}) async-start(s32[32,1,9]{2,1,0:T(1,128)} %bitcast.20), calls=%async_computation | async-start | bytes 32768 | tf_op jit(solution)/shard_map/all_to_all | solution.py:182
  43.9 285.2 %all-to-all-start.1 = ((bf16[32,9,64,256]{3,2,1,0:T(8,128)(2,1)}), bf16[32,9,64,256]{3,2,1,0:T(8,128)(2,1)}, u32[]{:S(2)}, u32[]{:S(2)}) async-start(bf16[32,9,64,256]{3,2,1,0:T(8,128)(2,1)} %bitcast.459), calls=%async_computation.1 | async-start | bytes 18874368 | tf_op jit(solution)/shard_map/all_to_all | solution.py:185
  51.4 273.7 %all-reduce.14.cloned.1.call-start = ((), (), s32[]{:S(2)}) async-start(), calls=%async_computation.3 | async-start | bytes 4194304 | tf_op jit(solution)/shard_map/psum | solution.py:18
  58.0 35.3 %collective-permute-start = (bf16[2,64,2048]{2,1,0:T(8,128)(2,1)}, bf16[2,64,2048]{2,1,0:T(8,128)(2,1)}, u32[]{:S(2)}, u32[]{:S(2)}) collective-permute-start(bf16[2,64,2048]{2,1,0:T(8,128)(2,1)} %get-tuple-element.342), channel_id=1, source_target_pairs={{0,1},{1,2},{2,3},{3,4},{4,5},{5,6},{6,7},{7,8},{8,9},{9,10},{10,1... | collective-permute-start | bytes 1572872 | tf_op jit(solution)/shard_map/ppermute | solution.py:29
  61.8 52.8 %collective-permute-start.1 = (bf16[2,64,2048]{2,1,0:T(8,128)(2,1)}, bf16[2,64,2048]{2,1,0:T(8,128)(2,1)}, u32[]{:S(2)}, u32[]{:S(2)}) collective-permute-start(bf16[2,64,2048]{2,1,0:T(8,128)(2,1)} %get-tuple-element.343), channel_id=1, source_target_pairs={{1,0},{2,1},{3,2},{4,3},{5,4},{6,5},{7,6},{8,7},{9,8},{10,9},{11,1... | collective-permute-start | bytes 1572872 | tf_op jit(solution)/shard_map/ppermute | solution.py:31
  355.9 3.7 copy-start.1
  380.2 3.8 copy-start.5
  427.7 3.7 copy-start.1
  452.0 3.8 copy-start.5
  499.5 3.7 copy-start.1
  523.8 3.8 copy-start.5
  526.0 3.0 copy-start
  571.3 3.7 copy-start.1
  595.6 3.8 copy-start.5
  660.3 4.9 copy-start.32
  694.3 6.1 copy-start.7
  694.3 6.1 copy-start.29
  694.3 579.3 %all-to-all-start.2 = ((bf16[32,9,64,256]{3,2,1,0:T(8,128)(2,1)}), bf16[32,9,64,256]{3,2,1,0:T(8,128)(2,1)}, u32[]{:S(2)}, u32[]{:S(2)}) async-start(bf16[32,9,64,256]{3,2,1,0:T(8,128)(2,1)} %bitcast.457), calls=%async_computation.2 | async-start | bytes 18874368 | tf_op jit(solution)/shard_map/all_to_all | solution.py:297
  700.3 432.0 %all-reduce.16.cloned.1.call-start = ((), (), s32[]{:S(2)}) async-start(), calls=%async_computation.4 | async-start | bytes 6291456 | tf_op jit(solution)/shard_map/psum | solution.py:253
  1019.5 5.5 slice-start.1
  1019.5 5.5 slice-start.2
  1026.9 293.5 %collective-permute-start.2 = (bf16[16,2,64,128]{3,0,1,2:T(8,128)(2,1)}, bf16[16,2,64,128]{3,0,1,2:T(8,128)(2,1)}, u32[]{:S(2)}, u32[]{:S(2)}) collective-permute-start(bf16[16,2,64,128]{3,0,1,2:T(8,128)(2,1)} %get-tuple-element.335), channel_id=1, source_target_pairs={{1,0},{2,1},{3,2},{4,3},{5,4},{6,5},{7,6},{8,7},{9,8},{10,9},{11,1... | collective-permute-start | bytes 1572872 | tf_op jit(solution)/shard_map/ppermute | solution.py:41
  1028.2 293.7 %collective-permute-start.3 = (bf16[16,2,64,128]{3,0,1,2:T(8,128)(2,1)}, bf16[16,2,64,128]{3,0,1,2:T(8,128)(2,1)}, u32[]{:S(2)}, u32[]{:S(2)}) collective-permute-start(bf16[16,2,64,128]{3,0,1,2:T(8,128)(2,1)} %get-tuple-element.334), channel_id=1, source_target_pairs={{0,1},{1,2},{2,3},{3,4},{4,5},{5,6},{6,7},{7,8},{8,9},{9,10},{10,1... | collective-permute-start | bytes 1572872 | tf_op jit(solution)/shard_map/ppermute | solution.py:41
  (65 other events, 121.0 us)
Sparse Core Ops, SparseCore 0:
  55.8 269.2 all-reduce.13
  956.7 175.5 all-reduce.15
where the time goes:
time: 1450 us; the launch traced here: 1440 us
  blocking collectives  538 us (37%)
  waiting for transfers between devices  353 us (24%)
  local copies, waits for them, and re-layouts  289 us (20%)
  matrix products  154 us (11%)
  other arithmetic  53.4 us (4%)
  starting transfers between devices  37.3 us (3%)
  between operations  14.9 us (1%)
    pmax x1, blocking collectives, shards(): edge_top = lax.pmax(jnp.max(edge_scores, axis=2), 'seq')  249 us
    psum x1, waiting for transfers between devices, broadcast(): return lax.psum(block, axis)  206 us
    psum x1, blocking collectives, shards(): edge_dquery_sum, global_sum = lax.psum((edge_dquery, global_part), 'seq')  123 us
    psum x1, blocking collectives, shards(): gain_grad = lax.psum(gain_term, ('dp', 'seq'))  106 us
    psum x1, waiting for transfers between devices, shards(): lax.psum((jnp.sum(edge_expo, axis=2), jnp.einsum('hqt,htd->hqd', edge_exp...  99.2 us
    psum x1, blocking collectives, shards(): lax.psum((jnp.sum(edge_expo, axis=2), jnp.einsum('hqt,htd->hqd', edge_exp...  59.2 us
    while x160, local copies, waits for them, and re-layouts  46.8 us
    dot_general x24, matrix products, spread_terms(): jnp.einsum('hpbc,hpbd->hpcd', coef_blocks[:, :, :, NG + offset], rows_in,...  41.4 us
  transfers between devices with their start and end apart: 9, of which 5 were waited for; matrix products, arithmetic and copies ran while one was open for 7% of the time, Pallas kernels for 0%

commit v1 on v0

--- a/solution.py
+++ b/solution.py
@@ -336,7 +336,7 @@
     gain_term = jnp.sum(key_eff_grad * to_heads(keys[0]).astype(jnp.float32), axis=(1, 2)).reshape(
         HEADS * HD
     )
-    gain_grad = lax.psum(gain_term, ("dp", "seq"))
+    gain_grad = lax.psum(lax.psum(gain_term, "seq"), "dp")
     return (
         from_heads(attended_all),
         from_heads(dquery_all),

time: 1450 us -> 1390 us (0.959)
  blocking collectives: 538 us -> 478 us
    psum x1, blocking collectives: 106 us -> 44.1 us  [shards(): gain_grad = lax.psum(lax.psum(gain_term, 'seq'), 'dp')]
    unnamed x58 -> x62, local copies, waits for them, and re-layouts: 33.7 us -> 34 us
where the time goes in v1:
time: 1390 us; the launch traced here: 1380 us
  blocking collectives  478 us (34%)
  waiting for transfers between devices  350 us (25%)
  local copies, waits for them, and re-layouts  288 us (21%)
  matrix products  154 us (11%)
  other arithmetic  53.3 us (4%)
  starting transfers between devices  37.2 us (3%)
  between operations  14.9 us (1%)
    pmax x1, blocking collectives, shards(): edge_top = lax.pmax(jnp.max(edge_scores, axis=2), 'seq')  248 us
    psum x1, waiting for transfers between devices, broadcast(): return lax.psum(block, axis)  203 us
    psum x1, blocking collectives, shards(): edge_dquery_sum, global_sum = lax.psum((edge_dquery, global_part), 'seq')  126 us
    psum x1, waiting for transfers between devices, shards(): lax.psum((jnp.sum(edge_expo, axis=2), jnp.einsum('hqt,htd->hqd', edge_exp...  98.6 us
    psum x1, blocking collectives, shards(): lax.psum((jnp.sum(edge_expo, axis=2), jnp.einsum('hqt,htd->hqd', edge_exp...  58.9 us
    while x160, local copies, waits for them, and re-layouts  46.8 us
    psum x1, blocking collectives, shards(): gain_grad = lax.psum(lax.psum(gain_term, 'seq'), 'dp')  44.1 us
    dot_general x24, matrix products, spread_terms(): jnp.einsum('hpbc,hpbd->hpcd', coef_blocks[:, :, :, NG + offset], rows_in,...  41.3 us
  transfers between devices with their start and end apart: 9, of which 5 were waited for; matrix products, arithmetic and copies ran while one was open for 7% of the time, Pallas kernels for 0%

profile of v1, /device:TPU:1, one launch (start us, length us, event | category | flops | bytes accessed | tf_op | source)
XLA Modules:
  0.0 1376.8 jit_solution(17663348680609651590)
XLA Ops:
  11.2 12.0 all-to-all-start
  33.7 10.3 gather_fusion
  43.9 7.5 all-to-all-start.1
  68.0 25.2 %collective-permute-done = bf16[2,64,2048]{2,1,0:T(8,128)(2,1)} collective-permute-done((bf16[2,64,2048]{2,1,0:T(8,128)(2,1)}, bf16[2,64,2048]{2,1,0:T(8,128)(2,1)}, u32[]{:S(2)}, u32[]{:S(2)}) %collective-permute-start) | collective-permute-done | bytes 524320 | tf_op jit(solution)/shard_map/ppermute | solution.py:29
  93.2 21.3 %collective-permute-done.1 = bf16[2,64,2048]{2,1,0:T(8,128)(2,1)} collective-permute-done((bf16[2,64,2048]{2,1,0:T(8,128)(2,1)}, bf16[2,64,2048]{2,1,0:T(8,128)(2,1)}, u32[]{:S(2)}, u32[]{:S(2)}) %collective-permute-start.1) | collective-permute-done | bytes 524320 | tf_op jit(solution)/shard_map/ppermute | solution.py:31
  119.1 203.4 %all-reduce.15.cloned.1.call-done = bf16[4,128,2048]{2,1,0:T(8,128)(2,1)} async-done(((bf16[4,128,2048]{2,1,0:T(8,128)(2,1)}), bf16[4,128,2048]{2,1,0:T(8,128)(2,1)}) %all-reduce.15.cloned.1.call-update) | async-done | bytes 2097168 | tf_op jit(solution)/shard_map/psum | solution.py:18
  326.4 11.8 gather_fusion.1
  338.2 8.1 fusion.134
  346.3 287.8 %while.24 = (s32[]{:T(128)}, bf16[4,4,4,64,128]{4,3,2,1,0:T(8,128)(2,1)}, bf16[4,4,4,64,128]{4,3,2,1,0:T(8,128)(2,1)}, f32[4,4,2,2,64,128]{5,1,0,2,4,3:T(4,128)}...) while((s32[]{:T(128)}, ...), condition=%wide.region_14.15_spmd.clone, body=%wide.region_10.14_spmd.clone.sunk | while | flops 952370176 | bytes 142396560 | solution.py:227
  366.3 5.2 bitcast_dynamic-update-slice_fusion.6
  438.1 5.2 bitcast_dynamic-update-slice_fusion.6
  509.8 5.2 bitcast_dynamic-update-slice_fusion.6
  634.1 12.7 copy.168
  646.7 10.8 reshape.529
  662.5 28.8 %scatter_fusion = bf16[288,64,256]{2,1,0:T(8,128)(2,1)} fusion(bf16[288,64,256]{2,1,0:T(8,128)(2,1)} %broadcast_in_dim.167, s32[192]{0:T(256)S(1)} %bitcast.510, bf16[192,64,256]{2,1,0:T(8,128)(2,1)} %reshape.529), kind=kCustom, calls=%fused_computation.3 | custom fusion | bytes 18875136 | tf_op jit(solution)/shard_map/scatter | solution.py:294
  691.2 5.9 all-to-all-start.2
  701.1 248.4 %pmax.7 = f32[16,128]{1,0:T(8,128)S(1)} all-reduce(f32[16,128]{1,0:T(8,128)S(1)} %get-tuple-element.354), channel_id=1, replica_groups=mesh['dp'=8,'seq'=32] {'seq'}, use_global_device_ids=true, to_apply=%region_2.3 | all-reduce | flops 2048 | bytes 16384 | tf_op jit(solution)/shard_map/pmax | solution.py:251
  956.9 58.9 %psum.51 = f32[16,128]{1,0:T(8,128)S(1)} all-reduce(f32[16,128]{1,0:T(8,128)S(1)} %fusion.95), channel_id=1, replica_groups=mesh['dp'=8,'seq'=32] {'seq'}, use_global_device_ids=true, to_apply=%region_5.6 | all-reduce | flops 2048 | bytes 16384 | tf_op jit(solution)/shard_map/psum | solution.py:253
  1029.5 98.6 %all-reduce.17.cloned.1.call-done = (f32[16,128,128]{2,1,0:T(8,128)}, f32[16,2,2,64,128]{4,0,1,3,2:T(8,128)}) async-done(((f32[16,128,128]{2,1,0:T(8,128)}, f32[16,2,2,64,128]{4,0,1,3,2:T(8,128)}), (f32[16,128,128]{2,1,0:T(8,128)}, f32[16,2,2,64,128]{4,0,1,3,2:T(8,128)})) %all-reduce.17.cloned.1.call-update) | async-done | bytes 3145744 | tf_op jit(solution)/shard_map/psum | solution.py:253
  1137.7 18.9 %copy.212 = bf16[36,8,64,256]{3,1,2,0:T(8,128)(2,1)} copy(bf16[36,8,64,256]{3,2,1,0:T(8,128)(2,1)} %bitcast.182) | data formatting | bytes 18874368
  1156.6 16.0 %dot_general.116 = bf16[64,2,128,288]{2,1,0,3:T(2,128)(2,1)} reshape(bf16[16384,288]{0,1:T(8,128)(2,1)} %bitcast.459) | data formatting | bytes 18874368 | tf_op jit(solution)/shard_map/dot_general | solution.py:302
  1172.6 12.3 fusion.85
  1191.1 126.3 %all-reduce.18 = (bf16[16,2,64,128]{3,2,1,0:T(8,128)(2,1)S(1)}, f32[2048]{0:T(1024)S(1)}) all-reduce(f32[16,2,64,128]{3,2,1,0:T(8,128)S(1)} %bitcast.484, f32[2048]{0:T(1024)S(1)} %bitcast.507), channel_id=1, replica_groups=mesh['dp'=8,'seq'=32] {'seq'}, use_global_device_ids=true, to_apply=%region_16.17 | all-reduce | flops 264192 | bytes 1589248 | tf_op jit(solution)/shard_map/psum | solution.py:312
  1325.7 44.1 %psum.55 = f32[2048]{0:T(1024)} all-reduce(f32[2048]{0:T(1024)S(1)} %get-tuple-element.315), channel_id=1, replica_groups=mesh['dp'=8,'seq'=32] {'dp'}, use_global_device_ids=true, to_apply=%region_21.22 | all-reduce | flops 2048 | bytes 16384 | tf_op jit(solution)/shard_map/psum | solution.py:339
  (481 shorter events, 363.4 us)
Async XLA Ops:
  9.3 58.6 %copy-start.33 = (s32[192,1]{0,1:T(1,128)}, s32[192,1]{0,1:T(1,128)S(1)}, u32[]{:S(2)}) copy-start(s32[192,1]{0,1:T(1,128)S(1)} %compare_select_fusion.1) | copy-start | bytes 2308
  11.2 20.6 %all-to-all-start = ((s32[32,1,9]{2,1,0:T(1,128)}), s32[32,1,9]{2,1,0:T(1,128)S(1)}, u32[]{:S(2)}, u32[]{:S(2)}) async-start(s32[32,1,9]{2,1,0:T(1,128)} %bitcast.20), calls=%async_computation | async-start | bytes 32768 | tf_op jit(solution)/shard_map/all_to_all | solution.py:182
  43.9 282.5 %all-to-all-start.1 = ((bf16[32,9,64,256]{3,2,1,0:T(8,128)(2,1)}), bf16[32,9,64,256]{3,2,1,0:T(8,128)(2,1)}, u32[]{:S(2)}, u32[]{:S(2)}) async-start(bf16[32,9,64,256]{3,2,1,0:T(8,128)(2,1)} %bitcast.458), calls=%async_computation.1 | async-start | bytes 18874368 | tf_op jit(solution)/shard_map/all_to_all | solution.py:185
  51.4 271.0 %all-reduce.15.cloned.1.call-start = ((), (), s32[]{:S(2)}) async-start(), calls=%async_computation.3 | async-start | bytes 4194304 | tf_op jit(solution)/shard_map/psum | solution.py:18
  57.9 35.3 %collective-permute-start = (bf16[2,64,2048]{2,1,0:T(8,128)(2,1)}, bf16[2,64,2048]{2,1,0:T(8,128)(2,1)}, u32[]{:S(2)}, u32[]{:S(2)}) collective-permute-start(bf16[2,64,2048]{2,1,0:T(8,128)(2,1)} %get-tuple-element.344), channel_id=1, source_target_pairs={{0,1},{1,2},{2,3},{3,4},{4,5},{5,6},{6,7},{7,8},{8,9},{9,10},{10,1... | collective-permute-start | bytes 1572872 | tf_op jit(solution)/shard_map/ppermute | solution.py:29
  61.8 52.7 %collective-permute-start.1 = (bf16[2,64,2048]{2,1,0:T(8,128)(2,1)}, bf16[2,64,2048]{2,1,0:T(8,128)(2,1)}, u32[]{:S(2)}, u32[]{:S(2)}) collective-permute-start(bf16[2,64,2048]{2,1,0:T(8,128)(2,1)} %get-tuple-element.345), channel_id=1, source_target_pairs={{1,0},{2,1},{3,2},{4,3},{5,4},{6,5},{7,6},{8,7},{9,8},{10,9},{11,1... | collective-permute-start | bytes 1572872 | tf_op jit(solution)/shard_map/ppermute | solution.py:31
  353.6 3.7 copy-start.1
  377.9 3.8 copy-start.5
  425.4 3.7 copy-start.1
  449.6 3.8 copy-start.5
  497.1 3.7 copy-start.1
  521.4 3.8 copy-start.5
  523.6 3.0 copy-start
  568.9 3.7 copy-start.1
  593.2 3.8 copy-start.5
  657.6 4.9 copy-start.34
  691.2 6.0 copy-start.7
  691.2 6.0 copy-start.31
  691.2 446.5 %all-to-all-start.2 = ((bf16[32,9,64,256]{3,2,1,0:T(8,128)(2,1)}), bf16[32,9,64,256]{3,2,1,0:T(8,128)(2,1)}, u32[]{:S(2)}, u32[]{:S(2)}) async-start(bf16[32,9,64,256]{3,2,1,0:T(8,128)(2,1)} %bitcast.456), calls=%async_computation.2 | async-start | bytes 18874368 | tf_op jit(solution)/shard_map/all_to_all | solution.py:297
  697.2 430.9 %all-reduce.17.cloned.1.call-start = ((), (), s32[]{:S(2)}) async-start(), calls=%async_computation.4 | async-start | bytes 6291456 | tf_op jit(solution)/shard_map/psum | solution.py:253
  1015.8 5.5 slice-start.1
  1015.8 5.5 slice-start.2
  1023.2 161.7 %collective-permute-start.2 = (bf16[16,2,64,128]{3,0,1,2:T(8,128)(2,1)}, bf16[16,2,64,128]{3,0,1,2:T(8,128)(2,1)}, u32[]{:S(2)}, u32[]{:S(2)}) collective-permute-start(bf16[16,2,64,128]{3,0,1,2:T(8,128)(2,1)} %get-tuple-element.337), channel_id=1, source_target_pairs={{1,0},{2,1},{3,2},{4,3},{5,4},{6,5},{7,6},{8,7},{9,8},{10,9},{11,1... | collective-permute-start | bytes 1572872 | tf_op jit(solution)/shard_map/ppermute | solution.py:41
  1024.5 161.9 %collective-permute-start.3 = (bf16[16,2,64,128]{3,0,1,2:T(8,128)(2,1)}, bf16[16,2,64,128]{3,0,1,2:T(8,128)(2,1)}, u32[]{:S(2)}, u32[]{:S(2)}) collective-permute-start(bf16[16,2,64,128]{3,0,1,2:T(8,128)(2,1)} %get-tuple-element.336), channel_id=1, source_target_pairs={{0,1},{1,2},{2,3},{3,4},{4,5},{5,6},{6,7},{7,8},{8,9},{9,10},{10,1... | collective-permute-start | bytes 1572872 | tf_op jit(solution)/shard_map/ppermute | solution.py:41
  (67 other events, 125.6 us)
Sparse Core Ops, SparseCore 0:
  55.8 266.6 all-reduce.14
  953.2 174.8 all-reduce.16
